TPU v7x, 32 devices: a whole 2x2x4 slice. The times are simulated.
32 devices in a mesh: gx: 4 (over y, x), gy: 4 (over z), gz: 2 (over core).
Axes of the slice: x: 2, y: 2, z: 4, core: 2. Of those that a mesh axis runs over, the one named last changes fastest.
Arguments:
- provisional: float32 [9, 128, 64, 256], P(None, 'gx', 'gy', 'gz'), may hold values from -6 to 6
- cut_flag: int32 [128, 64, 256], P('gx', 'gy', 'gz'), may hold values from 0 to 1, as said below
- cut_code: int32 [128, 64, 256], P('gx', 'gy', 'gz'), may hold values from 0 to 134217727
- volume_level: int32 [128, 64, 256], P('gx', 'gy', 'gz'), may hold values from 1 to 256
- area_level: int32 [128, 64, 256], P('gx', 'gy', 'gz'), may hold values from 64 to 256
Outputs:
- redistributed: float32 [9, 128, 64, 256], P(None, 'gx', 'gy', 'gz')
- species_change: float32 [9], replicated
Inputs may be any that keep to these rules, and one draw needn't show every extreme that they name: cut_flag marks the cells crossed by one closed embedded surface.
All inputs are finite; a program needn't handle non-finite values.
Results may differ from a plain program's by a relative error of at most 0.00002.
Values sent between devices are 32-bit elements; how exact they have to be, the bound alone decides.
A program may use at most 128 MiB of HBM per device.

v0:
```python
import math
import jax
import jax.numpy as jnp
from jax import lax
from jax.sharding import PartitionSpec as P

CENTER = 8192
OFFSETS = [(a, b, c) for a in (-1, 0, 1) for b in (-1, 0, 1) for c in (-1, 0, 1)]


def padded(cells, sides, width):
    for axis, dim in sides:
        count = lax.axis_size(axis)
        ends = count - 1
        head = lax.slice_in_dim(cells, 0, width, axis=dim)
        tail = lax.slice_in_dim(cells, cells.shape[dim] - width, cells.shape[dim], axis=dim)
        cells = jnp.concatenate(
            [
                lax.ppermute(tail, axis, [(i, (i + 1) % count) for i in range(ends)]),
                cells,
                lax.ppermute(head, axis, [((i + 1) % count, i) for i in range(ends)]),
            ],
            axis=dim,
        )
    return cells


def window(values, a, b, c, margin, border):
    extent_x = values.shape[-3] - 2 * border + 2 * margin
    extent_y = values.shape[-2] - 2 * border + 2 * margin
    extent_z = values.shape[-1] - 2 * border + 2 * margin
    start_x = border - margin + a
    start_y = border - margin + b
    start_z = border - margin + c
    return values[
        ...,
        start_x : start_x + extent_x,
        start_y : start_y + extent_y,
        start_z : start_z + extent_z,
    ]


def member(codes, position):
    return (codes >> position & 1).astype(jnp.float32)


def per_device(provisional, cut_flag, cut_code, volume_level, area_level):
    is_cut = cut_flag == 1
    stacked = jnp.stack(
        [
            jnp.where(is_cut, cut_code | CENTER, CENTER),
            jnp.where(is_cut, volume_level, 256),
            jnp.where(is_cut, area_level, 256),
        ]
    )
    border = 2
    grown = padded(stacked, (("gx", 1), ("gy", 2), ("gz", 3)), border)
    code_all = grown[0] | CENTER
    volume_all = grown[1].astype(jnp.float32) / 256.0
    face_all = grown[2].astype(jnp.float32) / 256.0
    margin = border - 1
    counted = jnp.zeros(window(code_all, 0, 0, 0, margin, border).shape, jnp.float32)
    for position, (a, b, c) in enumerate(OFFSETS):
        counted = counted + member(window(code_all, -a, -b, -c, margin, border), position)
    volume_near = window(volume_all, 0, 0, 0, margin, border)
    face_near = window(face_all, 0, 0, 0, margin, border)
    weights = volume_near / counted
    portions = volume_near * face_near / counted
    scaling = window(face_all, 0, 0, 0, 0, border) / window(counted, 0, 0, 0, 0, margin)
    volume_mid = window(volume_all, 0, 0, 0, 0, border)
    carried = padded(
        window(weights, 0, 0, 0, 0, 1)[None] * provisional, (("gx", 1), ("gy", 2), ("gz", 3)), 1
    )
    carry_border = 1
    inner_margin = 0
    code_inner = window(code_all, 0, 0, 0, inner_margin, border)
    beyond = (window(grown[1], 0, 0, 0, inner_margin, border) == 0).astype(jnp.float32)
    amounts = jnp.zeros(window(carried, 0, 0, 0, inner_margin, carry_border).shape, jnp.float32)
    gathered = jnp.zeros(code_inner.shape, jnp.float32)
    for position, (a, b, c) in enumerate(OFFSETS):
        present = member(code_inner, position)
        amounts = amounts + present * window(carried, a, b, c, inner_margin, carry_border)
        gathered = gathered + present * window(portions, a, b, c, inner_margin, margin)
    quotas = amounts / (gathered + beyond)
    quotas = padded(quotas, (("gx", 1), ("gy", 2), ("gz", 3)), 1)
    summed = jnp.zeros(provisional.shape, jnp.float32)
    for position, (a, b, c) in enumerate(OFFSETS):
        summed = summed + member(window(code_all, -a, -b, -c, 0, border), position) * window(
            quotas, -a, -b, -c, 0, 1
        )
    redistributed = scaling * summed
    cell_count = (
        provisional.shape[1]
        * provisional.shape[2]
        * provisional.shape[3]
        * lax.axis_size("gx")
        * lax.axis_size("gy")
        * lax.axis_size("gz")
    )
    local_sums = jnp.sum(volume_mid[None] * redistributed, axis=(1, 2, 3))
    species_change = lax.psum(local_sums, ("gx", "gy", "gz")) / math.sqrt(cell_count)
    return (redistributed, species_change)


def solution(mesh):
    in_specs = (
        P(None, "gx", "gy", "gz"),
        P("gx", "gy", "gz"),
        P("gx", "gy", "gz"),
        P("gx", "gy", "gz"),
        P("gx", "gy", "gz"),
    )
    out_specs = (P(None, "gx", "gy", "gz"), P())
    return jax.shard_map(
        per_device, mesh=mesh, in_specs=in_specs, out_specs=out_specs, check_vma=False
    )
```

profile of v0, /device:TPU:0, one launch (start us, length us, event | category | flops | bytes accessed | tf_op | source)
XLA Modules:
  0.0 276.7 jit_solution(5008713613444649050)
XLA Ops:
  2.8 4.9 %collective-permute-start = (s32[3,2,16,128]{3,2,1,0:T(8,128)S(1)}, s32[3,2,16,128]{3,2,1,0:T(8,128)S(1)}, u32[]{:S(2)}, u32[]{:S(2)}) collective-permute-start(s32[3,2,16,128]{3,2,1,0:T(8,128)S(1)} %get-tuple-element.91), channel_id=1, source_target_pairs={{0,8},{8,16},{16,24},{1,9},{9,17},{17,25},{2,10},{10,18},{18,26},{... | collective-permute-start | bytes 147464 | tf_op jit(solution)/shard_map/ppermute | solution.py:19
  7.7 1.3 collective-permute-start.1
  9.4 4.2 %collective-permute-done.1 = s32[3,2,16,128]{3,2,1,0:T(8,128)S(1)} collective-permute-done((s32[3,2,16,128]{3,2,1,0:T(8,128)S(1)}, s32[3,2,16,128]{3,2,1,0:T(8,128)S(1)}, u32[]{:S(2)}, u32[]{:S(2)}) %collective-permute-start.1) | collective-permute-done | bytes 49184 | tf_op jit(solution)/shard_map/ppermute | solution.py:21
  13.8 3.5 %collective-permute-start.2 = (s32[3,36,2,128]{3,2,1,0:T(2,128)S(1)}, s32[3,36,2,128]{3,2,1,0:T(2,128)S(1)}, u32[]{:S(2)}, u32[]{:S(2)}) collective-permute-start(s32[3,36,2,128]{3,2,1,0:T(2,128)S(1)} %get-tuple-element.87), channel_id=1, source_target_pairs={{0,2},{2,4},{4,6},{1,3},{3,5},{5,7},{8,10},{10,12},{12,14},{9,11},... | collective-permute-start | bytes 331784 | tf_op jit(solution)/shard_map/ppermute | solution.py:19
  17.3 1.3 collective-permute-start.3
  19.6 4.3 %collective-permute-done.3 = s32[3,36,2,128]{3,2,1,0:T(2,128)S(1)} collective-permute-done((s32[3,36,2,128]{3,2,1,0:T(2,128)S(1)}, s32[3,36,2,128]{3,2,1,0:T(2,128)S(1)}, u32[]{:S(2)}, u32[]{:S(2)}) %collective-permute-start.3) | collective-permute-done | bytes 110624 | tf_op jit(solution)/shard_map/ppermute | solution.py:21
  26.3 1.3 collective-permute-start.4
  28.2 1.3 collective-permute-start.5
  30.1 1.3 collective-permute-done.5
  31.4 1.5 copy.196
  32.9 4.2 %pad_add_fusion = s32[3,36,20,132]{3,2,1,0:T(8,128)S(1)} fusion(s32[3,36,20,2]{3,2,1,0:T(8,128)S(1)} %copy.196, s32[3,36,2,128]{3,2,1,0:T(2,128)} %copy-done.4, s32[3,2,16,128]{3,2,1,0:T(8,128)} %copy-done.6, s32[1,32,16,128]{3,2,1,0:T(8,128)S(1)} %get-tuple-element.94, s32[1,32,16,128]{3,2,1,0:T(8,128)S(1)} %get-tuple-element.93, ...), kind=kLoop, calls=%fused_computation.10 | loop fusion | flops 2280960 | bytes 2280960 | tf_op jit(solution)/shard_map/concatenate | solution.py:17
  37.6 3.0 %fusion.220 = (f32[32,16,128]{2,1,0:T(8,128)}, f32[32,16,128]{2,1,0:T(8,128)}, f32[32,16,128]{2,1,0:T(8,128)}, f32[32,16,128]{2,1,0:T(8,128)}, f32[32,16,128]{2,...) fusion(s32[36,20,132]{2,1,0:T(8,128)S(1)} %get-tuple-element.19), kind=kLoop, calls=%fused_computation.373 | loop fusion | flops 3735552 | bytes 5505024 | tf_op jit(solution)/shard_map/convert_element_type | solution.py:44
  40.6 4.8 %fusion.61 = (f32[34,18,130]{2,1,0:T(8,128)S(1)}, f32[34,18,130]{2,1,0:T(8,128)S(1)}) fusion(f32[36,20,132]{2,1,0:T(8,128)S(1)} %fusion.60, f32[36,20,132]{2,1,0:T(8,128)S(1)} %convert_multiply_fusion, s32[36,20,132]{2,1,0:T(8,128)S(1)} %get-tuple-element.19), kind=kLoop, calls=%fused_computation.132 | loop fusion | flops 8672040 | bytes 9865440 | tf_op jit(solution)/shard_map/div | solution.py:68
  46.6 4.3 %collective-permute-start.6 = (f32[9,1,16,128]{3,2,1,0:T(8,128)S(1)}, f32[9,1,16,128]{3,2,1,0:T(8,128)S(1)}, u32[]{:S(2)}, u32[]{:S(2)}) collective-permute-start(f32[9,1,16,128]{3,2,1,0:T(8,128)S(1)} %get-tuple-element.30), channel_id=1, source_target_pairs={{0,8},{8,16},{16,24},{1,9},{9,17},{17,25},{2,10},{10,18},{18,26},{... | collective-permute-start | bytes 221192 | tf_op jit(solution)/shard_map/ppermute | solution.py:19
  50.9 1.3 collective-permute-start.7
  52.2 2.3 fusion.193
  54.5 3.1 %fusion.191 = (f32[32,16,128]{2,1,0:T(8,128)}, f32[32,16,128]{2,1,0:T(8,128)}, f32[32,16,128]{2,1,0:T(8,128)}, f32[32,16,128]{2,1,0:T(8,128)}, f32[32,16,128]{2,...) fusion(s32[36,20,132]{2,1,0:T(8,128)S(1)} %get-tuple-element.19), kind=kLoop, calls=%fused_computation.314 | loop fusion | flops 3735552 | bytes 8126464 | tf_op jit(solution)/shard_map/convert_element_type | solution.py:44
  57.9 1.3 collective-permute-start.9
  59.2 4.7 %collective-permute-start.8 = (f32[9,34,1,128]{3,1,2,0:T(8,128)S(1)}, f32[9,34,1,128]{3,1,2,0:T(8,128)S(1)}, u32[]{:S(2)}, u32[]{:S(2)}) collective-permute-start(f32[9,34,1,128]{3,1,2,0:T(8,128)S(1)} %copy.197), channel_id=1, source_target_pairs={{0,2},{2,4},{4,6},{1,3},{3,5},{5,7},{8,10},{10,12},{12,14},{9,11},... | collective-permute-start | bytes 470024 | tf_op jit(solution)/shard_map/ppermute | solution.py:19
  63.9 3.0 %fusion.189 = (f32[32,16,128]{2,1,0:T(8,128)}, f32[32,16,128]{2,1,0:T(8,128)}, f32[32,16,128]{2,1,0:T(8,128)}, f32[32,16,128]{2,1,0:T(8,128)}, f32[32,16,128]{2,...) fusion(s32[36,20,132]{2,1,0:T(8,128)S(1)} %get-tuple-element.19), kind=kLoop, calls=%fused_computation.311 | loop fusion | flops 2949120 | bytes 7864320 | tf_op jit(solution)/shard_map/convert_element_type | solution.py:44
  68.4 4.2 %fusion.224 = (f32[9,34,18,1]{3,2,1,0:T(8,128)}, f32[9,34,18,1]{3,2,1,0:T(8,128)}) fusion(f32[9,34,18,128]{3,2,1,0:T(8,128)S(1)} %pad_maximum_fusion.2), kind=kLoop, calls=%fused_computation.422 | loop fusion | bytes 88128 | tf_op jit(solution)/shard_map/slice | solution.py:16
  72.6 3.5 %copy.201 = f32[9,34,18,1]{1,2,3,0:T(8,128)S(1)} copy(f32[9,34,18,1]{3,2,1,0:T(8,128)} %get-tuple-element.12) | data formatting | bytes 44064 | tf_op jit(solution)/shard_map/slice | solution.py:16
  76.1 3.5 %copy.204 = f32[9,34,18,1]{1,2,3,0:T(8,128)S(1)} copy(f32[9,34,18,1]{3,2,1,0:T(8,128)} %get-tuple-element.13) | data formatting | bytes 44064 | tf_op jit(solution)/shard_map/slice | solution.py:15
  79.7 1.3 collective-permute-start.11
  81.0 3.7 %collective-permute-start.10 = (f32[9,34,18,1]{1,2,3,0:T(8,128)S(1)}, f32[9,34,18,1]{1,2,3,0:T(8,128)}, u32[]{:S(2)}, u32[]{:S(2)}) collective-permute-start(f32[9,34,18,1]{1,2,3,0:T(8,128)S(1)} %copy.201), channel_id=1, source_target_pairs={{0,1},{2,3},{4,5},{6,7},{8,9},{10,11},{12,13},{14,15},{16,17},{18,... | collective-permute-start | bytes 66104 | tf_op jit(solution)/shard_map/ppermute | solution.py:19
  84.7 3.7 %maximum_maximum_fusion.2 = (f32[9,34,17,128]{3,2,1,0:T(8,128)}, f32[9,34,17,128]{3,2,1,0:T(8,128)}) fusion(f32[9,1,16,128]{3,2,1,0:T(8,128)S(1)} %collective-permute-done.7, f32[9,32,16,128]{3,2,1,0:T(8,128)S(1)} %broadcast_multiply_fusion, f32[9,1,16,128]{3,2,1,0:T(8,128)S(1)} %collective-permute-done.6, f32[9,34,1,128]{3,2,1,0:T(1,128)S(1)} %copy.199, ...), kind=kLoop, calls=%fused_computation.5 | loop fusion | flops 3995136 | bytes 8146944 | tf_op jit(solution)/shard_map/concatenate | solution.py:17
  88.4 3.9 %copy.202 = f32[9,34,18,1]{3,2,1,0:T(8,128)} copy(f32[9,34,18,1]{1,2,3,0:T(8,128)} %collective-permute-done.10) | data formatting | bytes 44064 | tf_op jit(solution)/shard_map/ppermute | solution.py:19
  92.3 3.2 %copy.205 = f32[9,34,18,1]{3,2,1,0:T(8,128)} copy(f32[9,34,18,1]{1,2,3,0:T(8,128)S(1)} %collective-permute-done.11) | data formatting | bytes 44064 | tf_op jit(solution)/shard_map/ppermute | solution.py:21
  95.5 10.9 %maximum_maximum_fusion = (f32[9,34,18,129]{3,2,1,0:T(8,128)S(1)}, f32[9,34,18,129]{3,2,1,0:T(8,128)}) fusion(f32[9,34,1,128]{3,2,1,0:T(1,128)S(1)} %copy.200, f32[9,1,16,128]{3,2,1,0:T(8,128)S(1)} %collective-permute-done.7, f32[9,32,16,128]{3,2,1,0:T(8,128)} %copy-done.1, f32[9,1,16,128]{3,2,1,0:T(8,128)S(1)} %collective-permute-done.6, ...), kind=kLoop, calls=%fused_computation | loop fusion | flops 7105320 | bytes 8548416 | tf_op jit(solution)/shard_map/concatenate | solution.py:17
  106.4 36.9 %fusion.30 = f32[9,32,16,128]{3,2,1,0:T(8,128)} fusion(f32[9,34,18,129]{3,2,1,0:T(8,128)} %get-tuple-element.17, f32[9,34,17,128]{3,2,1,0:T(8,128)} %get-tuple-element.25, f32[9,34,18,129]{3,2,1,0:T(8,128)S(1)} %get-tuple-element.16, f32[9,1,16,128]{3,2,1,0:T(8,128)S(1)} %collective-permute-done.7, f32[9,32,16,128]{3,2,1,0:T(8,128)} %copy-done.1, ...), kind=kLoop, calls=%fused_computation.68 | loop fusion | flops 33030144 | bytes 68829184 | tf_op jit(solution)/shard_map/div | solution.py:84
  144.3 4.4 %collective-permute-start.12 = (f32[9,1,16,128]{3,2,1,0:T(8,128)S(1)}, f32[9,1,16,128]{3,2,1,0:T(8,128)S(1)}, u32[]{:S(2)}, u32[]{:S(2)}) collective-permute-start(f32[9,1,16,128]{3,2,1,0:T(8,128)S(1)} %get-tuple-element.28), channel_id=1, source_target_pairs={{0,8},{8,16},{16,24},{1,9},{9,17},{17,25},{2,10},{10,18},{18,26},{... | collective-permute-start | bytes 221192 | tf_op jit(solution)/shard_map/ppermute | solution.py:19
  148.7 1.3 collective-permute-start.13
  150.7 4.3 %collective-permute-done.13 = f32[9,1,16,128]{3,2,1,0:T(8,128)S(1)} collective-permute-done((f32[9,1,16,128]{3,2,1,0:T(8,128)S(1)}, f32[9,1,16,128]{3,2,1,0:T(8,128)S(1)}, u32[]{:S(2)}, u32[]{:S(2)}) %collective-permute-start.13) | collective-permute-done | bytes 73760 | tf_op jit(solution)/shard_map/ppermute | solution.py:21
  155.0 1.9 pad_maximum_fusion.12
  156.9 1.3 collective-permute-start.15
  158.2 5.2 %collective-permute-start.14 = (f32[9,34,1,128]{3,1,2,0:T(8,128)S(1)}, f32[9,34,1,128]{3,1,2,0:T(8,128)S(1)}, u32[]{:S(2)}, u32[]{:S(2)}) collective-permute-start(f32[9,34,1,128]{3,1,2,0:T(8,128)S(1)} %copy.207), channel_id=1, source_target_pairs={{0,2},{2,4},{4,6},{1,3},{3,5},{5,7},{8,10},{10,12},{12,14},{9,11},... | collective-permute-start | bytes 470024 | tf_op jit(solution)/shard_map/ppermute | solution.py:19
  163.5 2.0 slice.847
  167.1 4.4 %fusion.223 = (f32[9,34,18,1]{3,2,1,0:T(8,128)}, f32[9,34,18,1]{3,2,1,0:T(8,128)}) fusion(f32[9,34,18,128]{3,2,1,0:T(8,128)S(1)} %pad_maximum_fusion.4), kind=kLoop, calls=%fused_computation.421 | loop fusion | bytes 88128 | tf_op jit(solution)/shard_map/slice | solution.py:15
  171.4 3.5 %copy.211 = f32[9,34,18,1]{1,2,3,0:T(8,128)S(1)} copy(f32[9,34,18,1]{3,2,1,0:T(8,128)} %get-tuple-element.10) | data formatting | bytes 44064 | tf_op jit(solution)/shard_map/slice | solution.py:15
  175.0 3.5 %copy.214 = f32[9,34,18,1]{1,2,3,0:T(8,128)S(1)} copy(f32[9,34,18,1]{3,2,1,0:T(8,128)} %get-tuple-element.11) | data formatting | bytes 44064 | tf_op jit(solution)/shard_map/slice | solution.py:16
  178.5 1.3 collective-permute-start.17
  179.8 1.3 collective-permute-start.16
  181.1 3.8 %pad_maximum_fusion.5 = (f32[9,34,17,128]{3,2,1,0:T(8,128)}, f32[9,34,17,128]{3,2,1,0:T(8,128)}) fusion(f32[9,34,1,128]{3,2,1,0:T(1,128)S(1)} %copy.210, f32[9,1,16,128]{3,2,1,0:T(8,128)S(1)} %collective-permute-done.13, f32[9,32,16,128]{3,2,1,0:T(8,128)S(1)} %copy-done, f32[9,1,16,128]{3,2,1,0:T(8,128)S(1)} %collective-permute-done.12, ...), kind=kLoop, calls=%fused_computation.8 | loop fusion | flops 3995136 | bytes 8146944 | tf_op jit(solution)/shard_map/concatenate | solution.py:17
  185.0 4.0 %copy.212 = f32[9,34,18,1]{3,2,1,0:T(8,128)} copy(f32[9,34,18,1]{1,2,3,0:T(8,128)} %collective-permute-done.16) | data formatting | bytes 44064 | tf_op jit(solution)/shard_map/ppermute | solution.py:21
  189.0 3.2 %copy.215 = f32[9,34,18,1]{3,2,1,0:T(8,128)} copy(f32[9,34,18,1]{1,2,3,0:T(8,128)S(1)} %collective-permute-done.17) | data formatting | bytes 44064 | tf_op jit(solution)/shard_map/ppermute | solution.py:19
  192.2 11.2 %pad_maximum_fusion.1 = (f32[9,34,18,129]{3,2,1,0:T(8,128)S(1)}, f32[9,34,18,129]{3,2,1,0:T(8,128)}) fusion(f32[9,34,18,1]{3,2,1,0:T(8,128)} %copy.212, f32[9,34,1,128]{3,2,1,0:T(1,128)S(1)} %copy.210, f32[9,1,16,128]{3,2,1,0:T(8,128)S(1)} %collective-permute-done.13, f32[9,32,16,128]{3,2,1,0:T(8,128)} %fusion.30, ...), kind=kLoop, calls=%fused_computation.2 | loop fusion | flops 7105320 | bytes 8548416 | tf_op jit(solution)/shard_map/concatenate | solution.py:17
  203.4 29.8 %multiply_reduce_fusion = (f32[9]{0:T(128)S(1)}, f32[9,32,16,128]{3,2,1,0:T(8,128)}) fusion(f32[32,16,128]{2,1,0:T(8,128)} %slice.847, f32[9,34,18,129]{3,2,1,0:T(8,128)} %get-tuple-element.15, f32[32,16,128]{2,1,0:T(8,128)} %get-tuple-element.62, f32[9,34,17,128]{3,2,1,0:T(8,128)} %get-tuple-element.21, f32[32,16,128]{2,1,0:T(8,128)} %get-tuple-element.63, ...), kind=kLoop, calls=%fused_computation.121 | loop fusion | flops 34209784 | bytes 69091360 | tf_op jit(solution)/shard_map/reduce_sum | solution.py:100
  233.2 43.0 %psum.7 = f32[9]{0:T(128)S(1)} all-reduce(f32[9]{0:T(128)S(1)} %get-tuple-element.4), channel_id=1, replica_groups=mesh['gx'=4,'gy'=4,'gz'=2] {'gx','gy','gz'}, use_global_device_ids=true, to_apply=%region_1.2 | all-reduce | flops 9 | bytes 72 | tf_op jit(solution)/shard_map/psum | solution.py:101
  (57 shorter events, 14.5 us)
Async XLA Ops:
  2.8 6.6 %collective-permute-start = (s32[3,2,16,128]{3,2,1,0:T(8,128)S(1)}, s32[3,2,16,128]{3,2,1,0:T(8,128)S(1)}, u32[]{:S(2)}, u32[]{:S(2)}) collective-permute-start(s32[3,2,16,128]{3,2,1,0:T(8,128)S(1)} %get-tuple-element.91), channel_id=1, source_target_pairs={{0,8},{8,16},{16,24},{1,9},{9,17},{17,25},{2,10},{10,18},{18,26},{... | collective-permute-start | bytes 147464 | tf_op jit(solution)/shard_map/ppermute | solution.py:19
  7.7 6.0 %collective-permute-start.1 = (s32[3,2,16,128]{3,2,1,0:T(8,128)S(1)}, s32[3,2,16,128]{3,2,1,0:T(8,128)S(1)}, u32[]{:S(2)}, u32[]{:S(2)}) collective-permute-start(s32[3,2,16,128]{3,2,1,0:T(8,128)S(1)} %get-tuple-element.92), channel_id=1, source_target_pairs={{8,0},{16,8},{24,16},{9,1},{17,9},{25,17},{10,2},{18,10},{26,18},{... | collective-permute-start | bytes 147464 | tf_op jit(solution)/shard_map/ppermute | solution.py:21
  9.4 14.5 %copy-start.5 = (s32[3,2,16,128]{3,2,1,0:T(8,128)}, s32[3,2,16,128]{3,2,1,0:T(8,128)S(1)}, u32[]{:S(2)}) copy-start(s32[3,2,16,128]{3,2,1,0:T(8,128)S(1)} %collective-permute-done) | copy-start | bytes 147460
  13.7 10.2 %copy-start.6 = (s32[3,2,16,128]{3,2,1,0:T(8,128)}, s32[3,2,16,128]{3,2,1,0:T(8,128)S(1)}, u32[]{:S(2)}) copy-start(s32[3,2,16,128]{3,2,1,0:T(8,128)S(1)} %collective-permute-done.1) | copy-start | bytes 147460
  13.8 5.8 %collective-permute-start.2 = (s32[3,36,2,128]{3,2,1,0:T(2,128)S(1)}, s32[3,36,2,128]{3,2,1,0:T(2,128)S(1)}, u32[]{:S(2)}, u32[]{:S(2)}) collective-permute-start(s32[3,36,2,128]{3,2,1,0:T(2,128)S(1)} %get-tuple-element.87), channel_id=1, source_target_pairs={{0,2},{2,4},{4,6},{1,3},{3,5},{5,7},{8,10},{10,12},{12,14},{9,11},... | collective-permute-start | bytes 331784 | tf_op jit(solution)/shard_map/ppermute | solution.py:19
  17.3 6.6 %collective-permute-start.3 = (s32[3,36,2,128]{3,2,1,0:T(2,128)S(1)}, s32[3,36,2,128]{3,2,1,0:T(2,128)S(1)}, u32[]{:S(2)}, u32[]{:S(2)}) collective-permute-start(s32[3,36,2,128]{3,2,1,0:T(2,128)S(1)} %get-tuple-element.88), channel_id=1, source_target_pairs={{2,0},{4,2},{6,4},{3,1},{5,3},{7,5},{10,8},{12,10},{14,12},{11,9},... | collective-permute-start | bytes 331784 | tf_op jit(solution)/shard_map/ppermute | solution.py:21
  23.9 0.6 copy-start.4
  26.3 3.1 %collective-permute-start.4 = (s32[3,36,20,2]{1,3,2,0:T(2,128)}, s32[3,36,20,2]{1,3,2,0:T(2,128)S(1)}, u32[]{:S(2)}, u32[]{:S(2)}) collective-permute-start(s32[3,36,20,2]{1,3,2,0:T(2,128)} %copy.193), channel_id=1, source_target_pairs={{0,1},{2,3},{4,5},{6,7},{8,9},{10,11},{12,13},{14,15},{16,17},{18,... | collective-permute-start | bytes 51848 | tf_op jit(solution)/shard_map/ppermute | solution.py:19
  28.2 3.3 %collective-permute-start.5 = (s32[3,36,20,2]{1,3,2,0:T(2,128)S(1)}, s32[3,36,20,2]{1,3,2,0:T(2,128)}, u32[]{:S(2)}, u32[]{:S(2)}) collective-permute-start(s32[3,36,20,2]{1,3,2,0:T(2,128)S(1)} %copy.194), channel_id=1, source_target_pairs={{1,0},{3,2},{5,4},{7,6},{9,8},{11,10},{13,12},{15,14},{17,16},{19,... | collective-permute-start | bytes 51848 | tf_op jit(solution)/shard_map/ppermute | solution.py:21
  37.2 3.5 %copy-start.2 = (f32[36,20,132]{2,1,0:T(8,128)}, f32[36,20,132]{2,1,0:T(8,128)S(1)}, u32[]{:S(2)}) copy-start(f32[36,20,132]{2,1,0:T(8,128)S(1)} %convert_multiply_fusion) | copy-start | bytes 1140484
  40.6 5.7 %copy-start.3 = (f32[9,32,16,128]{3,2,1,0:T(8,128)S(1)}, f32[9,32,16,128]{3,2,1,0:T(8,128)}, u32[]{:S(2)}) copy-start(f32[9,32,16,128]{3,2,1,0:T(8,128)} %param.5) | copy-start | bytes 7077892
  46.5 38.1 %copy-start.1 = (f32[9,32,16,128]{3,2,1,0:T(8,128)}, f32[9,32,16,128]{3,2,1,0:T(8,128)S(1)}, u32[]{:S(2)}) copy-start(f32[9,32,16,128]{3,2,1,0:T(8,128)S(1)} %broadcast_multiply_fusion) | copy-start | bytes 7077892
  46.6 11.0 %collective-permute-start.6 = (f32[9,1,16,128]{3,2,1,0:T(8,128)S(1)}, f32[9,1,16,128]{3,2,1,0:T(8,128)S(1)}, u32[]{:S(2)}, u32[]{:S(2)}) collective-permute-start(f32[9,1,16,128]{3,2,1,0:T(8,128)S(1)} %get-tuple-element.30), channel_id=1, source_target_pairs={{0,8},{8,16},{16,24},{1,9},{9,17},{17,25},{2,10},{10,18},{18,26},{... | collective-permute-start | bytes 221192 | tf_op jit(solution)/shard_map/ppermute | solution.py:19
  50.9 6.7 %collective-permute-start.7 = (f32[9,1,16,128]{3,2,1,0:T(8,128)S(1)}, f32[9,1,16,128]{3,2,1,0:T(8,128)S(1)}, u32[]{:S(2)}, u32[]{:S(2)}) collective-permute-start(f32[9,1,16,128]{3,2,1,0:T(8,128)S(1)} %get-tuple-element.31), channel_id=1, source_target_pairs={{8,0},{16,8},{24,16},{9,1},{17,9},{25,17},{10,2},{18,10},{26,18},{... | collective-permute-start | bytes 221192 | tf_op jit(solution)/shard_map/ppermute | solution.py:21
  57.9 9.1 %collective-permute-start.9 = (f32[9,34,1,128]{3,1,2,0:T(8,128)S(1)}, f32[9,34,1,128]{3,1,2,0:T(8,128)S(1)}, u32[]{:S(2)}, u32[]{:S(2)}) collective-permute-start(f32[9,34,1,128]{3,1,2,0:T(8,128)S(1)} %copy.198), channel_id=1, source_target_pairs={{2,0},{4,2},{6,4},{3,1},{5,3},{7,5},{10,8},{12,10},{14,12},{11,9},... | collective-permute-start | bytes 470024 | tf_op jit(solution)/shard_map/ppermute | solution.py:21
  59.2 8.5 %collective-permute-start.8 = (f32[9,34,1,128]{3,1,2,0:T(8,128)S(1)}, f32[9,34,1,128]{3,1,2,0:T(8,128)S(1)}, u32[]{:S(2)}, u32[]{:S(2)}) collective-permute-start(f32[9,34,1,128]{3,1,2,0:T(8,128)S(1)} %copy.197), channel_id=1, source_target_pairs={{0,2},{2,4},{4,6},{1,3},{3,5},{5,7},{8,10},{10,12},{12,14},{9,11},... | collective-permute-start | bytes 470024 | tf_op jit(solution)/shard_map/ppermute | solution.py:19
  79.7 12.6 %collective-permute-start.11 = (f32[9,34,18,1]{1,2,3,0:T(8,128)S(1)}, f32[9,34,18,1]{1,2,3,0:T(8,128)S(1)}, u32[]{:S(2)}, u32[]{:S(2)}) collective-permute-start(f32[9,34,18,1]{1,2,3,0:T(8,128)S(1)} %copy.204), channel_id=1, source_target_pairs={{1,0},{3,2},{5,4},{7,6},{9,8},{11,10},{13,12},{15,14},{17,16},{19,... | collective-permute-start | bytes 66104 | tf_op jit(solution)/shard_map/ppermute | solution.py:21
  81.0 7.4 %collective-permute-start.10 = (f32[9,34,18,1]{1,2,3,0:T(8,128)S(1)}, f32[9,34,18,1]{1,2,3,0:T(8,128)}, u32[]{:S(2)}, u32[]{:S(2)}) collective-permute-start(f32[9,34,18,1]{1,2,3,0:T(8,128)S(1)} %copy.201), channel_id=1, source_target_pairs={{0,1},{2,3},{4,5},{6,7},{8,9},{10,11},{12,13},{14,15},{16,17},{18,... | collective-permute-start | bytes 66104 | tf_op jit(solution)/shard_map/ppermute | solution.py:19
  144.3 22.1 %copy-start = (f32[9,32,16,128]{3,2,1,0:T(8,128)S(1)}, f32[9,32,16,128]{3,2,1,0:T(8,128)}, u32[]{:S(2)}) copy-start(f32[9,32,16,128]{3,2,1,0:T(8,128)} %fusion.30) | copy-start | bytes 7077892
  144.3 6.4 %collective-permute-start.12 = (f32[9,1,16,128]{3,2,1,0:T(8,128)S(1)}, f32[9,1,16,128]{3,2,1,0:T(8,128)S(1)}, u32[]{:S(2)}, u32[]{:S(2)}) collective-permute-start(f32[9,1,16,128]{3,2,1,0:T(8,128)S(1)} %get-tuple-element.28), channel_id=1, source_target_pairs={{0,8},{8,16},{16,24},{1,9},{9,17},{17,25},{2,10},{10,18},{18,26},{... | collective-permute-start | bytes 221192 | tf_op jit(solution)/shard_map/ppermute | solution.py:19
  148.7 6.2 %collective-permute-start.13 = (f32[9,1,16,128]{3,2,1,0:T(8,128)S(1)}, f32[9,1,16,128]{3,2,1,0:T(8,128)S(1)}, u32[]{:S(2)}, u32[]{:S(2)}) collective-permute-start(f32[9,1,16,128]{3,2,1,0:T(8,128)S(1)} %get-tuple-element.29), channel_id=1, source_target_pairs={{8,0},{16,8},{24,16},{9,1},{17,9},{25,17},{10,2},{18,10},{26,18},{... | collective-permute-start | bytes 221192 | tf_op jit(solution)/shard_map/ppermute | solution.py:21
  156.9 8.6 %collective-permute-start.15 = (f32[9,34,1,128]{3,1,2,0:T(8,128)S(1)}, f32[9,34,1,128]{3,1,2,0:T(8,128)S(1)}, u32[]{:S(2)}, u32[]{:S(2)}) collective-permute-start(f32[9,34,1,128]{3,1,2,0:T(8,128)S(1)} %copy.208), channel_id=1, source_target_pairs={{2,0},{4,2},{6,4},{3,1},{5,3},{7,5},{10,8},{12,10},{14,12},{11,9},... | collective-permute-start | bytes 470024 | tf_op jit(solution)/shard_map/ppermute | solution.py:21
  158.2 8.1 %collective-permute-start.14 = (f32[9,34,1,128]{3,1,2,0:T(8,128)S(1)}, f32[9,34,1,128]{3,1,2,0:T(8,128)S(1)}, u32[]{:S(2)}, u32[]{:S(2)}) collective-permute-start(f32[9,34,1,128]{3,1,2,0:T(8,128)S(1)} %copy.207), channel_id=1, source_target_pairs={{0,2},{2,4},{4,6},{1,3},{3,5},{5,7},{8,10},{10,12},{12,14},{9,11},... | collective-permute-start | bytes 470024 | tf_op jit(solution)/shard_map/ppermute | solution.py:19
  178.5 10.4 %collective-permute-start.17 = (f32[9,34,18,1]{1,2,3,0:T(8,128)S(1)}, f32[9,34,18,1]{1,2,3,0:T(8,128)S(1)}, u32[]{:S(2)}, u32[]{:S(2)}) collective-permute-start(f32[9,34,18,1]{1,2,3,0:T(8,128)S(1)} %copy.214), channel_id=1, source_target_pairs={{0,1},{2,3},{4,5},{6,7},{8,9},{10,11},{12,13},{14,15},{16,17},{18,... | collective-permute-start | bytes 66104 | tf_op jit(solution)/shard_map/ppermute | solution.py:19
  179.8 5.1 %collective-permute-start.16 = (f32[9,34,18,1]{1,2,3,0:T(8,128)S(1)}, f32[9,34,18,1]{1,2,3,0:T(8,128)}, u32[]{:S(2)}, u32[]{:S(2)}) collective-permute-start(f32[9,34,18,1]{1,2,3,0:T(8,128)S(1)} %copy.211), channel_id=1, source_target_pairs={{1,0},{3,2},{5,4},{7,6},{9,8},{11,10},{13,12},{15,14},{17,16},{19,... | collective-permute-start | bytes 66104 | tf_op jit(solution)/shard_map/ppermute | solution.py:21
where the time goes:
time: 278 us; the launch traced here: 277 us
  other arithmetic  124 us (45%)
  local copies, waits for them, and re-layouts  45.8 us (16%)
  starting transfers between devices  44.9 us (16%)
  blocking collectives  43 us (15%)
  waiting for transfers between devices  17.5 us (6%)
    psum x1, blocking collectives, per_device(): lax.psum(local_sums, ('gx', 'gy', 'gz')) / math.sqrt(cell_count)  43 us
    div x1, other arithmetic, per_device(): quotas = amounts / (gathered + beyond)  36.9 us
    concatenate x8, other arithmetic, padded(): jnp.concatenate([lax.ppermute(tail, axis, [(i, (i + 1) % count) for i in...  35.3 us
    ppermute x9, starting transfers between devices, padded(): lax.ppermute(tail, axis, [(i, (i + 1) % count) for i in range(ends)])  33.3 us
    reduce_sum x1, other arithmetic, per_device(): local_sums = jnp.sum(volume_mid[None] * redistributed, axis=(1, 2, 3))  29.8 us
    ppermute x9, waiting for transfers between devices, padded(): lax.ppermute(head, axis, [((i + 1) % count, i) for i in range(ends)])  14.2 us
    slice x9, local copies, waits for them, and re-layouts, padded(): lax.slice_in_dim(cells, cells.shape[dim] - width, cells.shape[dim], axis=...  13.8 us
    slice x6, local copies, waits for them, and re-layouts, padded(): head = lax.slice_in_dim(cells, 0, width, axis=dim)  12 us
  transfers between devices with their start and end apart: 18, of which 9 were waited for; matrix products, arithmetic and copies ran while one was open for 10% of the time, Pallas kernels for 0%

commit v1 on v0

--- a/solution.py
+++ b/solution.py
@@ -45,6 +45,12 @@
 
 
 def per_device(provisional, cut_flag, cut_code, volume_level, area_level):
+
+    def wait_body_in(xs):
+        for to_i in (("gy", "gz"), "gx"):
+            xs = lax.psum(xs, to_i)
+        return xs
+
     is_cut = cut_flag == 1
     stacked = jnp.stack(
         [
@@ -98,7 +104,7 @@
         * lax.axis_size("gz")
     )
     local_sums = jnp.sum(volume_mid[None] * redistributed, axis=(1, 2, 3))
-    species_change = lax.psum(local_sums, ("gx", "gy", "gz")) / math.sqrt(cell_count)
+    species_change = wait_body_in(local_sums) / math.sqrt(cell_count)
     return (redistributed, species_change)
 
 

time: 278 us -> 263 us (0.946)
  blocking collectives: 43 us -> 29.7 us
    psum x1 -> x2, blocking collectives: 43 us -> 29.7 us  [wait_body_in(): xs = lax.psum(xs, to_i)]
where the time goes in v1:
time: 263 us; the launch traced here: 262 us
  other arithmetic  123 us (47%)
  local copies, waits for them, and re-layouts  45.8 us (17%)
  starting transfers between devices  44.9 us (17%)
  blocking collectives  29.7 us (11%)
  waiting for transfers between devices  17.5 us (7%)
    div x1, other arithmetic, per_device(): quotas = amounts / (gathered + beyond)  36.5 us
    concatenate x8, other arithmetic, padded(): jnp.concatenate([lax.ppermute(tail, axis, [(i, (i + 1) % count) for i in...  35.2 us
    ppermute x9, starting transfers between devices, padded(): lax.ppermute(tail, axis, [(i, (i + 1) % count) for i in range(ends)])  33.3 us
    psum x2, blocking collectives, wait_body_in(): xs = lax.psum(xs, to_i)  29.7 us
    reduce_sum x1, other arithmetic, per_device(): local_sums = jnp.sum(volume_mid[None] * redistributed, axis=(1, 2, 3))  29.3 us
    ppermute x9, waiting for transfers between devices, padded(): lax.ppermute(head, axis, [((i + 1) % count, i) for i in range(ends)])  14.2 us
    slice x9, local copies, waits for them, and re-layouts, padded(): lax.slice_in_dim(cells, cells.shape[dim] - width, cells.shape[dim], axis=...  13.8 us
    slice x6, local copies, waits for them, and re-layouts, padded(): head = lax.slice_in_dim(cells, 0, width, axis=dim)  12 us
  transfers between devices with their start and end apart: 18, of which 9 were waited for; matrix products, arithmetic and copies ran while one was open for 10% of the time, Pallas kernels for 0%

profile of v1, /device:TPU:0, one launch (start us, length us, event | category | flops | bytes accessed | tf_op | source)
XLA Modules:
  0.0 262.4 jit_solution(8665359106191824397)
XLA Ops:
  2.8 4.9 %collective-permute-start = (s32[3,2,16,128]{3,2,1,0:T(8,128)S(1)}, s32[3,2,16,128]{3,2,1,0:T(8,128)S(1)}, u32[]{:S(2)}, u32[]{:S(2)}) collective-permute-start(s32[3,2,16,128]{3,2,1,0:T(8,128)S(1)} %get-tuple-element.91), channel_id=1, source_target_pairs={{0,8},{8,16},{16,24},{1,9},{9,17},{17,25},{2,10},{10,18},{18,26},{... | collective-permute-start | bytes 147464 | tf_op jit(solution)/shard_map/ppermute | solution.py:19
  7.7 1.3 collective-permute-start.1
  9.4 4.2 %collective-permute-done.1 = s32[3,2,16,128]{3,2,1,0:T(8,128)S(1)} collective-permute-done((s32[3,2,16,128]{3,2,1,0:T(8,128)S(1)}, s32[3,2,16,128]{3,2,1,0:T(8,128)S(1)}, u32[]{:S(2)}, u32[]{:S(2)}) %collective-permute-start.1) | collective-permute-done | bytes 49184 | tf_op jit(solution)/shard_map/ppermute | solution.py:21
  13.8 3.5 %collective-permute-start.2 = (s32[3,36,2,128]{3,2,1,0:T(2,128)S(1)}, s32[3,36,2,128]{3,2,1,0:T(2,128)S(1)}, u32[]{:S(2)}, u32[]{:S(2)}) collective-permute-start(s32[3,36,2,128]{3,2,1,0:T(2,128)S(1)} %get-tuple-element.87), channel_id=1, source_target_pairs={{0,2},{2,4},{4,6},{1,3},{3,5},{5,7},{8,10},{10,12},{12,14},{9,11},... | collective-permute-start | bytes 331784 | tf_op jit(solution)/shard_map/ppermute | solution.py:19
  17.3 1.3 collective-permute-start.3
  19.6 4.3 %collective-permute-done.3 = s32[3,36,2,128]{3,2,1,0:T(2,128)S(1)} collective-permute-done((s32[3,36,2,128]{3,2,1,0:T(2,128)S(1)}, s32[3,36,2,128]{3,2,1,0:T(2,128)S(1)}, u32[]{:S(2)}, u32[]{:S(2)}) %collective-permute-start.3) | collective-permute-done | bytes 110624 | tf_op jit(solution)/shard_map/ppermute | solution.py:21
  28.2 1.3 collective-permute-start.5
  30.1 1.3 collective-permute-done.5
  31.4 1.5 copy.196
  32.9 4.2 %pad_add_fusion = s32[3,36,20,132]{3,2,1,0:T(8,128)S(1)} fusion(s32[3,36,20,2]{3,2,1,0:T(8,128)S(1)} %copy.196, s32[3,36,2,128]{3,2,1,0:T(2,128)} %copy-done.4, s32[3,2,16,128]{3,2,1,0:T(8,128)} %copy-done.6, s32[1,32,16,128]{3,2,1,0:T(8,128)S(1)} %get-tuple-element.94, s32[1,32,16,128]{3,2,1,0:T(8,128)S(1)} %get-tuple-element.93, ...), kind=kLoop, calls=%fused_computation.10 | loop fusion | flops 2280960 | bytes 2280960 | tf_op jit(solution)/shard_map/concatenate | solution.py:17
  37.7 3.0 %fusion.220 = (f32[32,16,128]{2,1,0:T(8,128)}, f32[32,16,128]{2,1,0:T(8,128)}, f32[32,16,128]{2,1,0:T(8,128)}, f32[32,16,128]{2,1,0:T(8,128)}, f32[32,16,128]{2,...) fusion(s32[36,20,132]{2,1,0:T(8,128)S(1)} %get-tuple-element.19), kind=kLoop, calls=%fused_computation.373 | loop fusion | flops 3735552 | bytes 5505024 | tf_op jit(solution)/shard_map/convert_element_type | solution.py:44
  40.6 4.8 %fusion.61 = (f32[34,18,130]{2,1,0:T(8,128)S(1)}, f32[34,18,130]{2,1,0:T(8,128)S(1)}) fusion(f32[36,20,132]{2,1,0:T(8,128)S(1)} %fusion.60, f32[36,20,132]{2,1,0:T(8,128)S(1)} %convert_multiply_fusion, s32[36,20,132]{2,1,0:T(8,128)S(1)} %get-tuple-element.19), kind=kLoop, calls=%fused_computation.132 | loop fusion | flops 8672040 | bytes 9865440 | tf_op jit(solution)/shard_map/div | solution.py:74
  46.6 4.3 %collective-permute-start.6 = (f32[9,1,16,128]{3,2,1,0:T(8,128)S(1)}, f32[9,1,16,128]{3,2,1,0:T(8,128)S(1)}, u32[]{:S(2)}, u32[]{:S(2)}) collective-permute-start(f32[9,1,16,128]{3,2,1,0:T(8,128)S(1)} %get-tuple-element.30), channel_id=1, source_target_pairs={{0,8},{8,16},{16,24},{1,9},{9,17},{17,25},{2,10},{10,18},{18,26},{... | collective-permute-start | bytes 221192 | tf_op jit(solution)/shard_map/ppermute | solution.py:19
  50.9 1.3 collective-permute-start.7
  52.2 2.3 fusion.193
  54.5 3.1 %fusion.191 = (f32[32,16,128]{2,1,0:T(8,128)}, f32[32,16,128]{2,1,0:T(8,128)}, f32[32,16,128]{2,1,0:T(8,128)}, f32[32,16,128]{2,1,0:T(8,128)}, f32[32,16,128]{2,...) fusion(s32[36,20,132]{2,1,0:T(8,128)S(1)} %get-tuple-element.19), kind=kLoop, calls=%fused_computation.314 | loop fusion | flops 3735552 | bytes 8126464 | tf_op jit(solution)/shard_map/convert_element_type | solution.py:44
  57.9 1.3 collective-permute-start.9
  59.2 4.7 %collective-permute-start.8 = (f32[9,34,1,128]{3,1,2,0:T(8,128)S(1)}, f32[9,34,1,128]{3,1,2,0:T(8,128)S(1)}, u32[]{:S(2)}, u32[]{:S(2)}) collective-permute-start(f32[9,34,1,128]{3,1,2,0:T(8,128)S(1)} %copy.197), channel_id=1, source_target_pairs={{0,2},{2,4},{4,6},{1,3},{3,5},{5,7},{8,10},{10,12},{12,14},{9,11},... | collective-permute-start | bytes 470024 | tf_op jit(solution)/shard_map/ppermute | solution.py:19
  63.9 3.0 %fusion.189 = (f32[32,16,128]{2,1,0:T(8,128)}, f32[32,16,128]{2,1,0:T(8,128)}, f32[32,16,128]{2,1,0:T(8,128)}, f32[32,16,128]{2,1,0:T(8,128)}, f32[32,16,128]{2,...) fusion(s32[36,20,132]{2,1,0:T(8,128)S(1)} %get-tuple-element.19), kind=kLoop, calls=%fused_computation.311 | loop fusion | flops 2949120 | bytes 7864320 | tf_op jit(solution)/shard_map/convert_element_type | solution.py:44
  68.5 4.2 %fusion.224 = (f32[9,34,18,1]{3,2,1,0:T(8,128)}, f32[9,34,18,1]{3,2,1,0:T(8,128)}) fusion(f32[9,34,18,128]{3,2,1,0:T(8,128)S(1)} %pad_maximum_fusion.2), kind=kLoop, calls=%fused_computation.422 | loop fusion | bytes 88128 | tf_op jit(solution)/shard_map/slice | solution.py:16
  72.6 3.5 %copy.201 = f32[9,34,18,1]{1,2,3,0:T(8,128)S(1)} copy(f32[9,34,18,1]{3,2,1,0:T(8,128)} %get-tuple-element.12) | data formatting | bytes 44064 | tf_op jit(solution)/shard_map/slice | solution.py:16
  76.2 3.5 %copy.204 = f32[9,34,18,1]{1,2,3,0:T(8,128)S(1)} copy(f32[9,34,18,1]{3,2,1,0:T(8,128)} %get-tuple-element.13) | data formatting | bytes 44064 | tf_op jit(solution)/shard_map/slice | solution.py:15
  79.7 1.3 collective-permute-start.11
  81.0 3.7 %collective-permute-start.10 = (f32[9,34,18,1]{1,2,3,0:T(8,128)S(1)}, f32[9,34,18,1]{1,2,3,0:T(8,128)}, u32[]{:S(2)}, u32[]{:S(2)}) collective-permute-start(f32[9,34,18,1]{1,2,3,0:T(8,128)S(1)} %copy.201), channel_id=1, source_target_pairs={{0,1},{2,3},{4,5},{6,7},{8,9},{10,11},{12,13},{14,15},{16,17},{18,... | collective-permute-start | bytes 66104 | tf_op jit(solution)/shard_map/ppermute | solution.py:19
  84.7 3.8 %maximum_maximum_fusion.2 = (f32[9,34,17,128]{3,2,1,0:T(8,128)}, f32[9,34,17,128]{3,2,1,0:T(8,128)}) fusion(f32[9,1,16,128]{3,2,1,0:T(8,128)S(1)} %collective-permute-done.7, f32[9,32,16,128]{3,2,1,0:T(8,128)S(1)} %broadcast_multiply_fusion, f32[9,1,16,128]{3,2,1,0:T(8,128)S(1)} %collective-permute-done.6, f32[9,34,1,128]{3,2,1,0:T(1,128)S(1)} %copy.199, ...), kind=kLoop, calls=%fused_computation.5 | loop fusion | flops 3995136 | bytes 8146944 | tf_op jit(solution)/shard_map/concatenate | solution.py:17
  88.5 3.9 %copy.202 = f32[9,34,18,1]{3,2,1,0:T(8,128)} copy(f32[9,34,18,1]{1,2,3,0:T(8,128)} %collective-permute-done.10) | data formatting | bytes 44064 | tf_op jit(solution)/shard_map/ppermute | solution.py:19
  92.4 3.2 %copy.205 = f32[9,34,18,1]{3,2,1,0:T(8,128)} copy(f32[9,34,18,1]{1,2,3,0:T(8,128)S(1)} %collective-permute-done.11) | data formatting | bytes 44064 | tf_op jit(solution)/shard_map/ppermute | solution.py:21
  95.6 10.9 %maximum_maximum_fusion = (f32[9,34,18,129]{3,2,1,0:T(8,128)S(1)}, f32[9,34,18,129]{3,2,1,0:T(8,128)}) fusion(f32[9,34,1,128]{3,2,1,0:T(1,128)S(1)} %copy.200, f32[9,1,16,128]{3,2,1,0:T(8,128)S(1)} %collective-permute-done.7, f32[9,32,16,128]{3,2,1,0:T(8,128)} %copy-done.1, f32[9,1,16,128]{3,2,1,0:T(8,128)S(1)} %collective-permute-done.6, ...), kind=kLoop, calls=%fused_computation | loop fusion | flops 7105320 | bytes 8548416 | tf_op jit(solution)/shard_map/concatenate | solution.py:17
  106.5 36.5 %fusion.30 = f32[9,32,16,128]{3,2,1,0:T(8,128)} fusion(f32[9,34,18,129]{3,2,1,0:T(8,128)} %get-tuple-element.17, f32[9,34,17,128]{3,2,1,0:T(8,128)} %get-tuple-element.25, f32[9,34,18,129]{3,2,1,0:T(8,128)S(1)} %get-tuple-element.16, f32[9,1,16,128]{3,2,1,0:T(8,128)S(1)} %collective-permute-done.7, f32[9,32,16,128]{3,2,1,0:T(8,128)} %copy-done.1, ...), kind=kLoop, calls=%fused_computation.68 | loop fusion | flops 33030144 | bytes 68829184 | tf_op jit(solution)/shard_map/div | solution.py:90
  144.0 4.4 %collective-permute-start.12 = (f32[9,1,16,128]{3,2,1,0:T(8,128)S(1)}, f32[9,1,16,128]{3,2,1,0:T(8,128)S(1)}, u32[]{:S(2)}, u32[]{:S(2)}) collective-permute-start(f32[9,1,16,128]{3,2,1,0:T(8,128)S(1)} %get-tuple-element.28), channel_id=1, source_target_pairs={{0,8},{8,16},{16,24},{1,9},{9,17},{17,25},{2,10},{10,18},{18,26},{... | collective-permute-start | bytes 221192 | tf_op jit(solution)/shard_map/ppermute | solution.py:19
  148.4 1.3 collective-permute-start.13
  150.4 4.3 %collective-permute-done.13 = f32[9,1,16,128]{3,2,1,0:T(8,128)S(1)} collective-permute-done((f32[9,1,16,128]{3,2,1,0:T(8,128)S(1)}, f32[9,1,16,128]{3,2,1,0:T(8,128)S(1)}, u32[]{:S(2)}, u32[]{:S(2)}) %collective-permute-start.13) | collective-permute-done | bytes 73760 | tf_op jit(solution)/shard_map/ppermute | solution.py:21
  154.6 1.9 pad_maximum_fusion.12
  156.6 1.3 collective-permute-start.15
  157.9 5.2 %collective-permute-start.14 = (f32[9,34,1,128]{3,1,2,0:T(8,128)S(1)}, f32[9,34,1,128]{3,1,2,0:T(8,128)S(1)}, u32[]{:S(2)}, u32[]{:S(2)}) collective-permute-start(f32[9,34,1,128]{3,1,2,0:T(8,128)S(1)} %copy.207), channel_id=1, source_target_pairs={{0,2},{2,4},{4,6},{1,3},{3,5},{5,7},{8,10},{10,12},{12,14},{9,11},... | collective-permute-start | bytes 470024 | tf_op jit(solution)/shard_map/ppermute | solution.py:19
  163.1 2.0 slice.847
  166.7 4.3 %fusion.223 = (f32[9,34,18,1]{3,2,1,0:T(8,128)}, f32[9,34,18,1]{3,2,1,0:T(8,128)}) fusion(f32[9,34,18,128]{3,2,1,0:T(8,128)S(1)} %pad_maximum_fusion.4), kind=kLoop, calls=%fused_computation.421 | loop fusion | bytes 88128 | tf_op jit(solution)/shard_map/slice | solution.py:15
  171.1 3.5 %copy.211 = f32[9,34,18,1]{1,2,3,0:T(8,128)S(1)} copy(f32[9,34,18,1]{3,2,1,0:T(8,128)} %get-tuple-element.10) | data formatting | bytes 44064 | tf_op jit(solution)/shard_map/slice | solution.py:15
  174.6 3.5 %copy.214 = f32[9,34,18,1]{1,2,3,0:T(8,128)S(1)} copy(f32[9,34,18,1]{3,2,1,0:T(8,128)} %get-tuple-element.11) | data formatting | bytes 44064 | tf_op jit(solution)/shard_map/slice | solution.py:16
  178.2 1.3 collective-permute-start.17
  179.5 1.3 collective-permute-start.16
  180.8 3.8 %pad_maximum_fusion.5 = (f32[9,34,17,128]{3,2,1,0:T(8,128)}, f32[9,34,17,128]{3,2,1,0:T(8,128)}) fusion(f32[9,34,1,128]{3,2,1,0:T(1,128)S(1)} %copy.210, f32[9,1,16,128]{3,2,1,0:T(8,128)S(1)} %collective-permute-done.13, f32[9,32,16,128]{3,2,1,0:T(8,128)S(1)} %copy-done, f32[9,1,16,128]{3,2,1,0:T(8,128)S(1)} %collective-permute-done.12, ...), kind=kLoop, calls=%fused_computation.8 | loop fusion | flops 3995136 | bytes 8146944 | tf_op jit(solution)/shard_map/concatenate | solution.py:17
  184.6 4.0 %copy.212 = f32[9,34,18,1]{3,2,1,0:T(8,128)} copy(f32[9,34,18,1]{1,2,3,0:T(8,128)} %collective-permute-done.16) | data formatting | bytes 44064 | tf_op jit(solution)/shard_map/ppermute | solution.py:21
  188.6 3.2 %copy.215 = f32[9,34,18,1]{3,2,1,0:T(8,128)} copy(f32[9,34,18,1]{1,2,3,0:T(8,128)S(1)} %collective-permute-done.17) | data formatting | bytes 44064 | tf_op jit(solution)/shard_map/ppermute | solution.py:19
  191.8 11.0 %pad_maximum_fusion.1 = (f32[9,34,18,129]{3,2,1,0:T(8,128)S(1)}, f32[9,34,18,129]{3,2,1,0:T(8,128)}) fusion(f32[9,34,18,1]{3,2,1,0:T(8,128)} %copy.212, f32[9,34,1,128]{3,2,1,0:T(1,128)S(1)} %copy.210, f32[9,1,16,128]{3,2,1,0:T(8,128)S(1)} %collective-permute-done.13, f32[9,32,16,128]{3,2,1,0:T(8,128)} %fusion.30, ...), kind=kLoop, calls=%fused_computation.2 | loop fusion | flops 7105320 | bytes 8548416 | tf_op jit(solution)/shard_map/concatenate | solution.py:17
  202.8 29.3 %multiply_reduce_fusion = (f32[9]{0:T(128)S(1)}, f32[9,32,16,128]{3,2,1,0:T(8,128)}) fusion(f32[32,16,128]{2,1,0:T(8,128)} %slice.847, f32[9,34,18,129]{3,2,1,0:T(8,128)} %get-tuple-element.15, f32[32,16,128]{2,1,0:T(8,128)} %get-tuple-element.62, f32[9,34,17,128]{3,2,1,0:T(8,128)} %get-tuple-element.21, f32[32,16,128]{2,1,0:T(8,128)} %get-tuple-element.63, ...), kind=kLoop, calls=%fused_computation.121 | loop fusion | flops 34209784 | bytes 69091360 | tf_op jit(solution)/shard_map/reduce_sum | solution.py:106
  232.1 19.9 %psum.14 = f32[9]{0:T(128)S(1)} all-reduce(f32[9]{0:T(128)S(1)} %get-tuple-element.4), channel_id=1, replica_groups=mesh['gx'=4,'gy'=4,'gz'=2] {'gy','gz'}, use_global_device_ids=true, to_apply=%region_1.2 | all-reduce | flops 9 | bytes 72 | tf_op jit(solution)/shard_map/psum | solution.py:51
  252.0 9.8 %psum.15 = f32[9]{0:T(128)S(1)} all-reduce(f32[9]{0:T(128)S(1)} %psum.14), channel_id=1, replica_groups=mesh['gx'=4,'gy'=4,'gz'=2] {'gx'}, use_global_device_ids=true, to_apply=%region_2.3 | all-reduce | flops 9 | bytes 72 | tf_op jit(solution)/shard_map/psum | solution.py:51
  (58 shorter events, 15.8 us)
Async XLA Ops:
  2.8 6.6 %collective-permute-start = (s32[3,2,16,128]{3,2,1,0:T(8,128)S(1)}, s32[3,2,16,128]{3,2,1,0:T(8,128)S(1)}, u32[]{:S(2)}, u32[]{:S(2)}) collective-permute-start(s32[3,2,16,128]{3,2,1,0:T(8,128)S(1)} %get-tuple-element.91), channel_id=1, source_target_pairs={{0,8},{8,16},{16,24},{1,9},{9,17},{17,25},{2,10},{10,18},{18,26},{... | collective-permute-start | bytes 147464 | tf_op jit(solution)/shard_map/ppermute | solution.py:19
  7.7 6.0 %collective-permute-start.1 = (s32[3,2,16,128]{3,2,1,0:T(8,128)S(1)}, s32[3,2,16,128]{3,2,1,0:T(8,128)S(1)}, u32[]{:S(2)}, u32[]{:S(2)}) collective-permute-start(s32[3,2,16,128]{3,2,1,0:T(8,128)S(1)} %get-tuple-element.92), channel_id=1, source_target_pairs={{8,0},{16,8},{24,16},{9,1},{17,9},{25,17},{10,2},{18,10},{26,18},{... | collective-permute-start | bytes 147464 | tf_op jit(solution)/shard_map/ppermute | solution.py:21
  9.4 14.5 %copy-start.5 = (s32[3,2,16,128]{3,2,1,0:T(8,128)}, s32[3,2,16,128]{3,2,1,0:T(8,128)S(1)}, u32[]{:S(2)}) copy-start(s32[3,2,16,128]{3,2,1,0:T(8,128)S(1)} %collective-permute-done) | copy-start | bytes 147460
  13.7 10.2 %copy-start.6 = (s32[3,2,16,128]{3,2,1,0:T(8,128)}, s32[3,2,16,128]{3,2,1,0:T(8,128)S(1)}, u32[]{:S(2)}) copy-start(s32[3,2,16,128]{3,2,1,0:T(8,128)S(1)} %collective-permute-done.1) | copy-start | bytes 147460
  13.8 5.8 %collective-permute-start.2 = (s32[3,36,2,128]{3,2,1,0:T(2,128)S(1)}, s32[3,36,2,128]{3,2,1,0:T(2,128)S(1)}, u32[]{:S(2)}, u32[]{:S(2)}) collective-permute-start(s32[3,36,2,128]{3,2,1,0:T(2,128)S(1)} %get-tuple-element.87), channel_id=1, source_target_pairs={{0,2},{2,4},{4,6},{1,3},{3,5},{5,7},{8,10},{10,12},{12,14},{9,11},... | collective-permute-start | bytes 331784 | tf_op jit(solution)/shard_map/ppermute | solution.py:19
  17.3 6.6 %collective-permute-start.3 = (s32[3,36,2,128]{3,2,1,0:T(2,128)S(1)}, s32[3,36,2,128]{3,2,1,0:T(2,128)S(1)}, u32[]{:S(2)}, u32[]{:S(2)}) collective-permute-start(s32[3,36,2,128]{3,2,1,0:T(2,128)S(1)} %get-tuple-element.88), channel_id=1, source_target_pairs={{2,0},{4,2},{6,4},{3,1},{5,3},{7,5},{10,8},{12,10},{14,12},{11,9},... | collective-permute-start | bytes 331784 | tf_op jit(solution)/shard_map/ppermute | solution.py:21
  23.9 0.6 copy-start.4
  26.3 3.1 %collective-permute-start.4 = (s32[3,36,20,2]{1,3,2,0:T(2,128)}, s32[3,36,20,2]{1,3,2,0:T(2,128)S(1)}, u32[]{:S(2)}, u32[]{:S(2)}) collective-permute-start(s32[3,36,20,2]{1,3,2,0:T(2,128)} %copy.193), channel_id=1, source_target_pairs={{0,1},{2,3},{4,5},{6,7},{8,9},{10,11},{12,13},{14,15},{16,17},{18,... | collective-permute-start | bytes 51848 | tf_op jit(solution)/shard_map/ppermute | solution.py:19
  28.2 3.3 %collective-permute-start.5 = (s32[3,36,20,2]{1,3,2,0:T(2,128)S(1)}, s32[3,36,20,2]{1,3,2,0:T(2,128)}, u32[]{:S(2)}, u32[]{:S(2)}) collective-permute-start(s32[3,36,20,2]{1,3,2,0:T(2,128)S(1)} %copy.194), channel_id=1, source_target_pairs={{1,0},{3,2},{5,4},{7,6},{9,8},{11,10},{13,12},{15,14},{17,16},{19,... | collective-permute-start | bytes 51848 | tf_op jit(solution)/shard_map/ppermute | solution.py:21
  37.2 3.5 %copy-start.2 = (f32[36,20,132]{2,1,0:T(8,128)}, f32[36,20,132]{2,1,0:T(8,128)S(1)}, u32[]{:S(2)}) copy-start(f32[36,20,132]{2,1,0:T(8,128)S(1)} %convert_multiply_fusion) | copy-start | bytes 1140484
  40.6 5.7 %copy-start.3 = (f32[9,32,16,128]{3,2,1,0:T(8,128)S(1)}, f32[9,32,16,128]{3,2,1,0:T(8,128)}, u32[]{:S(2)}) copy-start(f32[9,32,16,128]{3,2,1,0:T(8,128)} %param.5) | copy-start | bytes 7077892
  46.6 38.2 %copy-start.1 = (f32[9,32,16,128]{3,2,1,0:T(8,128)}, f32[9,32,16,128]{3,2,1,0:T(8,128)S(1)}, u32[]{:S(2)}) copy-start(f32[9,32,16,128]{3,2,1,0:T(8,128)S(1)} %broadcast_multiply_fusion) | copy-start | bytes 7077892
  46.6 11.0 %collective-permute-start.6 = (f32[9,1,16,128]{3,2,1,0:T(8,128)S(1)}, f32[9,1,16,128]{3,2,1,0:T(8,128)S(1)}, u32[]{:S(2)}, u32[]{:S(2)}) collective-permute-start(f32[9,1,16,128]{3,2,1,0:T(8,128)S(1)} %get-tuple-element.30), channel_id=1, source_target_pairs={{0,8},{8,16},{16,24},{1,9},{9,17},{17,25},{2,10},{10,18},{18,26},{... | collective-permute-start | bytes 221192 | tf_op jit(solution)/shard_map/ppermute | solution.py:19
  50.9 6.7 %collective-permute-start.7 = (f32[9,1,16,128]{3,2,1,0:T(8,128)S(1)}, f32[9,1,16,128]{3,2,1,0:T(8,128)S(1)}, u32[]{:S(2)}, u32[]{:S(2)}) collective-permute-start(f32[9,1,16,128]{3,2,1,0:T(8,128)S(1)} %get-tuple-element.31), channel_id=1, source_target_pairs={{8,0},{16,8},{24,16},{9,1},{17,9},{25,17},{10,2},{18,10},{26,18},{... | collective-permute-start | bytes 221192 | tf_op jit(solution)/shard_map/ppermute | solution.py:21
  57.9 9.1 %collective-permute-start.9 = (f32[9,34,1,128]{3,1,2,0:T(8,128)S(1)}, f32[9,34,1,128]{3,1,2,0:T(8,128)S(1)}, u32[]{:S(2)}, u32[]{:S(2)}) collective-permute-start(f32[9,34,1,128]{3,1,2,0:T(8,128)S(1)} %copy.198), channel_id=1, source_target_pairs={{2,0},{4,2},{6,4},{3,1},{5,3},{7,5},{10,8},{12,10},{14,12},{11,9},... | collective-permute-start | bytes 470024 | tf_op jit(solution)/shard_map/ppermute | solution.py:21
  59.2 8.5 %collective-permute-start.8 = (f32[9,34,1,128]{3,1,2,0:T(8,128)S(1)}, f32[9,34,1,128]{3,1,2,0:T(8,128)S(1)}, u32[]{:S(2)}, u32[]{:S(2)}) collective-permute-start(f32[9,34,1,128]{3,1,2,0:T(8,128)S(1)} %copy.197), channel_id=1, source_target_pairs={{0,2},{2,4},{4,6},{1,3},{3,5},{5,7},{8,10},{10,12},{12,14},{9,11},... | collective-permute-start | bytes 470024 | tf_op jit(solution)/shard_map/ppermute | solution.py:19
  79.7 12.7 %collective-permute-start.11 = (f32[9,34,18,1]{1,2,3,0:T(8,128)S(1)}, f32[9,34,18,1]{1,2,3,0:T(8,128)S(1)}, u32[]{:S(2)}, u32[]{:S(2)}) collective-permute-start(f32[9,34,18,1]{1,2,3,0:T(8,128)S(1)} %copy.204), channel_id=1, source_target_pairs={{1,0},{3,2},{5,4},{7,6},{9,8},{11,10},{13,12},{15,14},{17,16},{19,... | collective-permute-start | bytes 66104 | tf_op jit(solution)/shard_map/ppermute | solution.py:21
  81.0 7.5 %collective-permute-start.10 = (f32[9,34,18,1]{1,2,3,0:T(8,128)S(1)}, f32[9,34,18,1]{1,2,3,0:T(8,128)}, u32[]{:S(2)}, u32[]{:S(2)}) collective-permute-start(f32[9,34,18,1]{1,2,3,0:T(8,128)S(1)} %copy.201), channel_id=1, source_target_pairs={{0,1},{2,3},{4,5},{6,7},{8,9},{10,11},{12,13},{14,15},{16,17},{18,... | collective-permute-start | bytes 66104 | tf_op jit(solution)/shard_map/ppermute | solution.py:19
  144.0 22.1 %copy-start = (f32[9,32,16,128]{3,2,1,0:T(8,128)S(1)}, f32[9,32,16,128]{3,2,1,0:T(8,128)}, u32[]{:S(2)}) copy-start(f32[9,32,16,128]{3,2,1,0:T(8,128)} %fusion.30) | copy-start | bytes 7077892
  144.0 6.4 %collective-permute-start.12 = (f32[9,1,16,128]{3,2,1,0:T(8,128)S(1)}, f32[9,1,16,128]{3,2,1,0:T(8,128)S(1)}, u32[]{:S(2)}, u32[]{:S(2)}) collective-permute-start(f32[9,1,16,128]{3,2,1,0:T(8,128)S(1)} %get-tuple-element.28), channel_id=1, source_target_pairs={{0,8},{8,16},{16,24},{1,9},{9,17},{17,25},{2,10},{10,18},{18,26},{... | collective-permute-start | bytes 221192 | tf_op jit(solution)/shard_map/ppermute | solution.py:19
  148.4 6.2 %collective-permute-start.13 = (f32[9,1,16,128]{3,2,1,0:T(8,128)S(1)}, f32[9,1,16,128]{3,2,1,0:T(8,128)S(1)}, u32[]{:S(2)}, u32[]{:S(2)}) collective-permute-start(f32[9,1,16,128]{3,2,1,0:T(8,128)S(1)} %get-tuple-element.29), channel_id=1, source_target_pairs={{8,0},{16,8},{24,16},{9,1},{17,9},{25,17},{10,2},{18,10},{26,18},{... | collective-permute-start | bytes 221192 | tf_op jit(solution)/shard_map/ppermute | solution.py:21
  156.6 8.6 %collective-permute-start.15 = (f32[9,34,1,128]{3,1,2,0:T(8,128)S(1)}, f32[9,34,1,128]{3,1,2,0:T(8,128)S(1)}, u32[]{:S(2)}, u32[]{:S(2)}) collective-permute-start(f32[9,34,1,128]{3,1,2,0:T(8,128)S(1)} %copy.208), channel_id=1, source_target_pairs={{2,0},{4,2},{6,4},{3,1},{5,3},{7,5},{10,8},{12,10},{14,12},{11,9},... | collective-permute-start | bytes 470024 | tf_op jit(solution)/shard_map/ppermute | solution.py:21
  157.9 8.1 %collective-permute-start.14 = (f32[9,34,1,128]{3,1,2,0:T(8,128)S(1)}, f32[9,34,1,128]{3,1,2,0:T(8,128)S(1)}, u32[]{:S(2)}, u32[]{:S(2)}) collective-permute-start(f32[9,34,1,128]{3,1,2,0:T(8,128)S(1)} %copy.207), channel_id=1, source_target_pairs={{0,2},{2,4},{4,6},{1,3},{3,5},{5,7},{8,10},{10,12},{12,14},{9,11},... | collective-permute-start | bytes 470024 | tf_op jit(solution)/shard_map/ppermute | solution.py:19
  178.2 10.4 %collective-permute-start.17 = (f32[9,34,18,1]{1,2,3,0:T(8,128)S(1)}, f32[9,34,18,1]{1,2,3,0:T(8,128)S(1)}, u32[]{:S(2)}, u32[]{:S(2)}) collective-permute-start(f32[9,34,18,1]{1,2,3,0:T(8,128)S(1)} %copy.214), channel_id=1, source_target_pairs={{0,1},{2,3},{4,5},{6,7},{8,9},{10,11},{12,13},{14,15},{16,17},{18,... | collective-permute-start | bytes 66104 | tf_op jit(solution)/shard_map/ppermute | solution.py:19
  179.5 5.1 %collective-permute-start.16 = (f32[9,34,18,1]{1,2,3,0:T(8,128)S(1)}, f32[9,34,18,1]{1,2,3,0:T(8,128)}, u32[]{:S(2)}, u32[]{:S(2)}) collective-permute-start(f32[9,34,18,1]{1,2,3,0:T(8,128)S(1)} %copy.211), channel_id=1, source_target_pairs={{1,0},{3,2},{5,4},{7,6},{9,8},{11,10},{13,12},{15,14},{17,16},{19,... | collective-permute-start | bytes 66104 | tf_op jit(solution)/shard_map/ppermute | solution.py:21
